TPU v7x, 256 devices: a whole 4x4x8 slice. The times are simulated.
256 devices in a mesh: tm: 128 (over x_hi, z, y, core), mp: 2 (over x_lo).
Axes of the slice: x: 4 (x_hi: 2, x_lo: 2; x = x_hi * 2 + x_lo), y: 4, z: 8, core: 2. Of those that a mesh axis runs over, the one named last changes fastest.
Arguments:
- latent_picture_tokens: bfloat16 [256, 384, 768], P(('tm', 'mp')), may hold values from -6 to 6
- mixing_rescale_factor: float32 [2, 768], replicated, may hold values from 0.1 to 1.9
- joint_lookup_matrix: bfloat16 [2, 768, 1280], P(None, None, 'mp')
- score_scaling: float32 [2, 6], replicated, may hold values from 1 to 24
- mixing_return_matrix: bfloat16 [2, 768, 768], P(None, 'mp'), may hold values from -0.21875 to 0.21875
- perceptron_rescale_factor: float32 [2, 768], replicated, may hold values from 0.1 to 1.9
- widening_matrix: bfloat16 [2, 768, 1536], P(None, None, 'mp'), may hold values from -0.21875 to 0.21875
- narrowing_matrix: bfloat16 [2, 1536, 768], P(None, 'mp'), may hold values from -0.15625 to 0.15625
Outputs:
- result: bfloat16 [256, 384, 768], P(('tm', 'mp'))
All inputs are finite; a program needn't handle non-finite values.
Results may differ from a plain program's by a relative error of at most 0.033.
Values may be sent and summed in bfloat16 or wider, within the bound.
No kernel may reach another device: no remote copies, remote signals or barrier semaphores. Data moves between devices by JAX's collectives and lax.ppermute only.
A program may use at most 128 MiB of HBM per device.

v0:
```python
import math

import jax
import jax.numpy as jnp
from jax import lax
from jax.sharding import PartitionSpec as P

HEAD_SIZE = 128
ASKERS_IN_GROUP = 3
S = 384


def from_everyone(value, axis):
    copies = jnp.broadcast_to(value, (lax.axis_size(axis), *value.shape))
    return lax.all_to_all(copies, axis, split_axis=0, concat_axis=0, tiled=True)


def in_order(blocks, dim):
    blocks = jnp.moveaxis(blocks, 0, dim)
    dims = blocks.shape
    return blocks.reshape(*dims[:dim], dims[dim] * dims[dim + 1], *dims[dim + 2 :])


def collect(value, axis, dim):
    blocks = from_everyone(value, axis)
    return in_order(blocks, dim)


def passed_along(value, axis, by):
    size = lax.axis_size(axis)
    pairs = [(i, i + by) for i in range(size) if 0 <= i + by < size]
    return lax.ppermute(value, axis, pairs)


def from_root(value, axis, root):
    mine = lax.axis_index(axis) == root
    return lax.psum(jnp.where(mine, value, jnp.zeros_like(value)), axis)


def rms_rows(x, gain):
    content_vectors = x.astype(jnp.float32)
    scale = lax.rsqrt(jnp.mean(content_vectors * content_vectors, axis=-1, keepdims=True) + 1e-06)
    return content_vectors * scale * gain


def head_norm(t):
    return t * lax.rsqrt(jnp.mean(t * t, axis=-1, keepdims=True) + 1e-06)


def separate_subspaces(flat_vectors, groups, temps):
    count = flat_vectors.shape[0]
    reshaped_rows = flat_vectors.reshape(count, S, groups, ASKERS_IN_GROUP + 2, HEAD_SIZE)
    asker_vectors = (
        head_norm(reshaped_rows[:, :, :, :ASKERS_IN_GROUP, :])
        * temps[None, None, :, :, None]
        / math.sqrt(HEAD_SIZE)
    )
    matcher_vectors = head_norm(reshaped_rows[:, :, :, ASKERS_IN_GROUP, :])
    content_vectors = reshaped_rows[:, :, :, ASKERS_IN_GROUP + 1, :]
    return (
        asker_vectors.astype(jnp.bfloat16),
        matcher_vectors.astype(jnp.bfloat16),
        content_vectors.astype(jnp.bfloat16),
    )


def attend(
    asker_vectors, matcher_vectors, content_vectors, prior_k, prior_v, anchor_k, anchor_v, frame_ids
):
    own = jnp.einsum(
        "fsgrd,ftgd->fgrst", asker_vectors, matcher_vectors, preferred_element_type=jnp.float32
    )
    prior = jnp.einsum(
        "fsgrd,ftgd->fgrst", asker_vectors, prior_k, preferred_element_type=jnp.float32
    )
    anchor = jnp.einsum(
        "fsgrd,tgd->fgrst", asker_vectors, anchor_k, preferred_element_type=jnp.float32
    )
    lowest = jnp.float32(-1e30)
    prior = jnp.where((frame_ids >= 1)[:, None, None, None, None], prior, lowest)
    anchor = jnp.where((frame_ids >= 2)[:, None, None, None, None], anchor, lowest)
    top = jnp.maximum(
        jnp.maximum(jnp.max(own, axis=-1, keepdims=True), jnp.max(prior, axis=-1, keepdims=True)),
        jnp.max(anchor, axis=-1, keepdims=True),
    )
    e_own = jnp.exp(own - top)
    e_prior = jnp.exp(prior - top)
    e_anchor = jnp.exp(anchor - top)
    total = (
        jnp.sum(e_own, axis=-1, keepdims=True)
        + jnp.sum(e_prior, axis=-1, keepdims=True)
        + jnp.sum(e_anchor, axis=-1, keepdims=True)
    )
    p_own = (e_own / total).astype(jnp.bfloat16)
    p_prior = (e_prior / total).astype(jnp.bfloat16)
    p_anchor = (e_anchor / total).astype(jnp.bfloat16)
    mixed = jnp.einsum(
        "fgrst,ftgd->fsgrd", p_own, content_vectors, preferred_element_type=jnp.float32
    )
    mixed = mixed + jnp.einsum(
        "fgrst,ftgd->fsgrd", p_prior, prior_v, preferred_element_type=jnp.float32
    )
    mixed = mixed + jnp.einsum(
        "fgrst,tgd->fsgrd", p_anchor, anchor_v, preferred_element_type=jnp.float32
    )
    count = asker_vectors.shape[0]
    return mixed.astype(jnp.bfloat16).reshape(count, S, -1)


def layer_by_weights(state, gain_attn, qkv_local, temps, out_local, gain_ffn, up_local, down_local):
    count = state.shape[0]
    normed = rms_rows(state, gain_attn).astype(jnp.bfloat16)
    flat_vectors = jnp.einsum(
        "fsd,dc->fsc", normed, collect(qkv_local, "mp", 1), preferred_element_type=jnp.float32
    )
    groups = flat_vectors.shape[2] // ((ASKERS_IN_GROUP + 2) * HEAD_SIZE)
    asker_vectors, matcher_vectors, content_vectors = separate_subspaces(
        flat_vectors, groups, temps.reshape(-1, ASKERS_IN_GROUP)
    )
    edge_k, edge_v = passed_along(
        (matcher_vectors[count - 1], content_vectors[count - 1]), ("tm", "mp"), 1
    )
    prior_k = jnp.concatenate([edge_k[None], matcher_vectors[: count - 1]], axis=0)
    prior_v = jnp.concatenate([edge_v[None], content_vectors[: count - 1]], axis=0)
    anchor_k, anchor_v = (
        from_root(matcher_vectors[0], ("tm", "mp"), 0),
        from_root(content_vectors[0], ("tm", "mp"), 0),
    )
    frame_ids = lax.axis_index(("tm", "mp")) * count + jnp.arange(count, dtype=jnp.int32)
    heads_out = attend(
        asker_vectors,
        matcher_vectors,
        content_vectors,
        prior_k,
        prior_v,
        anchor_k,
        anchor_v,
        frame_ids,
    )
    block = heads_out
    mixed = jnp.einsum(
        "fsc,cd->fsd", block, collect(out_local, "mp", 0), preferred_element_type=jnp.float32
    )
    state = (state.astype(jnp.float32) + mixed).astype(jnp.bfloat16)
    normed2 = rms_rows(state, gain_ffn).astype(jnp.bfloat16)
    hidden = jnp.einsum(
        "fsd,dc->fsc", normed2, collect(up_local, "mp", 1), preferred_element_type=jnp.float32
    )
    active = jax.nn.gelu(hidden, approximate=True).astype(jnp.bfloat16)
    block = active
    update = jnp.einsum(
        "fsc,cd->fsd", block, collect(down_local, "mp", 0), preferred_element_type=jnp.float32
    )
    return (state.astype(jnp.float32) + update).astype(jnp.bfloat16)


def shards(
    latent_picture_tokens,
    mixing_rescale_factor,
    joint_lookup_matrix,
    score_scaling,
    mixing_return_matrix,
    perceptron_rescale_factor,
    widening_matrix,
    narrowing_matrix,
):
    state = latent_picture_tokens
    for depth_position in range(joint_lookup_matrix.shape[0]):
        state = layer_by_weights(
            state,
            mixing_rescale_factor[depth_position],
            joint_lookup_matrix[depth_position],
            score_scaling[depth_position],
            mixing_return_matrix[depth_position],
            perceptron_rescale_factor[depth_position],
            widening_matrix[depth_position],
            narrowing_matrix[depth_position],
        )
    return state


def solution(mesh):
    in_specs = (
        P(("tm", "mp"), None, None),
        P(),
        P(None, None, "mp"),
        P(),
        P(None, "mp", None),
        P(),
        P(None, None, "mp"),
        P(None, "mp", None),
    )
    out_specs = P(("tm", "mp"), None, None)
    return jax.shard_map(shards, mesh=mesh, in_specs=in_specs, out_specs=out_specs, check_vma=False)
```

profile of v0, /device:TPU:8, one launch (start us, length us, event | category | flops | bytes accessed | tf_op | source)
XLA Modules:
  0.0 776.9 jit_solution(12823817386249610233)
XLA Ops:
  10.3 4.9 all-to-all-start
  28.3 10.6 %all-to-all-done = bf16[2,768,640]{1,2,0:T(8,128)(2,1)} async-done(((bf16[2,768,640]{1,2,0:T(8,128)(2,1)}), bf16[2,768,640]{1,2,0:T(8,128)(2,1)}, u32[]{:S(2)}, u32[]{:S(2)}) %all-to-all-start) | async-done | bytes 1966112 | tf_op jit(solution)/shard_map/all_to_all | solution.py:15
  40.1 4.5 all-to-all-start.1
  44.7 2.8 convolution_bitcast_fusion.1
  49.5 3.9 collective-permute-start
  57.9 253.0 %all-reduce.7.cloned.1.call-done = (bf16[384,2,128]{0,2,1:T(8,128)(2,1)}, bf16[384,2,128]{0,2,1:T(8,128)(2,1)}) async-done(((bf16[384,2,128]{0,2,1:T(8,128)(2,1)}, bf16[384,2,128]{0,2,1:T(8,128)(2,1)}), (bf16[384,2,128]{0,2,1:T(8,128)(2,1)}, bf16[384,2,128]{0,2,1:T(8,128)(2,1)})) %all-reduce.7.cloned.1.call-update) | async-done | bytes 393232 | tf_op jit(solution)/shard_map/psum | solution.py:37
  310.9 3.6 bitcast_reduce_fusion.3
  314.6 3.4 bitcast_reduce_fusion.4
  321.4 5.0 all-to-all-start.2
  326.4 4.7 fusion.8
  334.6 20.1 %all-to-all-done.2 = bf16[2,768,768]{1,2,0:T(8,128)(2,1)} async-done(((bf16[2,768,768]{1,2,0:T(8,128)(2,1)}), bf16[2,768,768]{1,2,0:T(8,128)(2,1)}, u32[]{:S(2)}, u32[]{:S(2)}) %all-to-all-start.2) | async-done | bytes 2359328 | tf_op jit(solution)/shard_map/all_to_all | solution.py:15
  354.7 2.9 broadcast_in_dim.84
  357.7 5.3 all-to-all-start.3
  366.6 2.9 fusion.85
  369.5 20.8 %all-to-all-done.3 = bf16[2,768,768]{2,1,0:T(8,128)(2,1)} async-done(((bf16[2,768,768]{2,1,0:T(8,128)(2,1)}), bf16[2,768,768]{2,1,0:T(8,128)(2,1)}, u32[]{:S(2)}, u32[]{:S(2)}) %all-to-all-start.3) | async-done | bytes 2359328 | tf_op jit(solution)/shard_map/all_to_all | solution.py:15
  391.7 3.9 all-to-all-start.4
  395.6 5.0 fusion.88
  400.6 17.2 %all-to-all-done.4 = bf16[2,768,640]{1,2,0:T(8,128)(2,1)S(1)} async-done(((bf16[2,768,640]{1,2,0:T(8,128)(2,1)}), bf16[2,768,640]{1,2,0:T(8,128)(2,1)S(1)}, u32[]{:S(2)}, u32[]{:S(2)}) %all-to-all-start.4) | async-done | bytes 1966112 | tf_op jit(solution)/shard_map/all_to_all | solution.py:15
  419.0 4.5 all-to-all-start.5
  423.5 2.8 convolution_bitcast_fusion
  428.3 3.9 collective-permute-start.2
  436.8 248.6 %all-reduce.5.cloned.1.call-done = (bf16[384,2,128]{0,2,1:T(8,128)(2,1)}, bf16[384,2,128]{0,2,1:T(8,128)(2,1)}) async-done(((bf16[384,2,128]{0,2,1:T(8,128)(2,1)}, bf16[384,2,128]{0,2,1:T(8,128)(2,1)}), (bf16[384,2,128]{0,2,1:T(8,128)(2,1)}, bf16[384,2,128]{0,2,1:T(8,128)(2,1)})) %all-reduce.5.cloned.1.call-update) | async-done | bytes 393232 | tf_op jit(solution)/shard_map/psum | solution.py:37
  685.3 3.6 bitcast_reduce_fusion
  689.0 3.4 bitcast_reduce_fusion.1
  695.8 5.0 all-to-all-start.6
  700.9 4.7 fusion.10
  706.2 2.8 fusion.32
  709.0 20.1 %all-to-all-done.6 = bf16[2,768,768]{1,2,0:T(8,128)(2,1)} async-done(((bf16[2,768,768]{1,2,0:T(8,128)(2,1)}), bf16[2,768,768]{1,2,0:T(8,128)(2,1)}, u32[]{:S(2)}, u32[]{:S(2)}) %all-to-all-start.6) | async-done | bytes 2359328 | tf_op jit(solution)/shard_map/all_to_all | solution.py:15
  729.1 2.9 broadcast_in_dim.88
  732.1 5.4 all-to-all-start.7
  743.1 21.5 %all-to-all-done.7 = bf16[2,768,768]{2,1,0:T(8,128)(2,1)} async-done(((bf16[2,768,768]{2,1,0:T(8,128)(2,1)}), bf16[2,768,768]{2,1,0:T(8,128)(2,1)}, u32[]{:S(2)}, u32[]{:S(2)}) %all-to-all-start.7) | async-done | bytes 2359328 | tf_op jit(solution)/shard_map/all_to_all | solution.py:15
  764.7 5.4 fusion.81
  (126 shorter events, 53.7 us)
Async XLA Ops:
  10.3 4.9 copy-start.22
  10.3 28.7 %all-to-all-start = ((bf16[2,768,640]{1,2,0:T(8,128)(2,1)}), bf16[2,768,640]{1,2,0:T(8,128)(2,1)}, u32[]{:S(2)}, u32[]{:S(2)}) async-start(bf16[2,768,640]{1,2,0:T(8,128)(2,1)} %broadcast_in_dim.42), calls=%async_computation | async-start | bytes 3932160 | tf_op jit(solution)/shard_map/all_to_all | solution.py:15
  21.8 4.9 copy-start.11
  28.3 16.4 %copy-start.14 = (bf16[1,384,768]{2,1,0:T(8,128)(2,1)S(1)}, bf16[1,384,768]{2,1,0:T(8,128)(2,1)}, u32[]{:S(2)}) copy-start(bf16[1,384,768]{2,1,0:T(8,128)(2,1)} %param.8) | copy-start | bytes 1769476
  40.1 278.4 %all-to-all-start.1 = ((bf16[2,384,768]{2,1,0:T(8,128)(2,1)}), bf16[2,384,768]{2,1,0:T(8,128)(2,1)}, u32[]{:S(2)}, u32[]{:S(2)}) async-start(bf16[2,384,768]{2,1,0:T(8,128)(2,1)} %broadcast_in_dim.82), calls=%async_computation.1 | async-start | bytes 2359296 | tf_op jit(solution)/shard_map/all_to_all | solution.py:15
  44.6 266.3 %all-reduce.7.cloned.1.call-start = ((), (), s32[]{:S(2)}) async-start(), calls=%async_computation.9 | async-start | bytes 786432 | tf_op jit(solution)/shard_map/psum | solution.py:37
  47.5 7.8 %copy-start.9 = (f32[1,384,2,5,128]{1,4,3,2,0:T(8,128)}, f32[1,384,2,5,128]{1,4,3,2,0:T(8,128)S(1)}, u32[]{:S(2)}) copy-start(f32[1,384,2,5,128]{1,4,3,2,0:T(8,128)S(1)} %convolution_bitcast_fusion.1) | copy-start | bytes 5898244
  49.5 265.1 %collective-permute-start = (bf16[384,2,128]{0,2,1:T(8,128)(2,1)}, bf16[384,2,128]{0,2,1:T(8,128)(2,1)}, u32[]{:S(2)}, u32[]{:S(2)}) collective-permute-start(bf16[384,2,128]{0,2,1:T(8,128)(2,1)} %get-tuple-element.28), channel_id=1, source_target_pairs={{0,1},{1,2},{2,3},{3,4},{4,5},{5,6},{6,7},{7,8},{8,9},{9,10},{10,1... | collective-permute-start | bytes 589832 | tf_op jit(solution)/shard_map/ppermute | solution.py:32
  53.3 309.7 %collective-permute-start.1 = (bf16[384,2,128]{0,2,1:T(8,128)(2,1)}, bf16[384,2,128]{0,2,1:T(8,128)(2,1)}, u32[]{:S(2)}, u32[]{:S(2)}) collective-permute-start(bf16[384,2,128]{0,2,1:T(8,128)(2,1)} %get-tuple-element.26), channel_id=1, source_target_pairs={{0,1},{1,2},{2,3},{3,4},{4,5},{5,6},{6,7},{7,8},{8,9},{9,10},{10,1... | collective-permute-start | bytes 589832 | tf_op jit(solution)/shard_map/ppermute | solution.py:32
  310.9 3.6 copy-start.5
  321.4 5.0 copy-start.17
  321.4 33.3 %all-to-all-start.2 = ((bf16[2,768,768]{1,2,0:T(8,128)(2,1)}), bf16[2,768,768]{1,2,0:T(8,128)(2,1)}, u32[]{:S(2)}, u32[]{:S(2)}) async-start(bf16[2,768,768]{1,2,0:T(8,128)(2,1)} %broadcast_in_dim.83), calls=%async_computation.2 | async-start | bytes 4718592 | tf_op jit(solution)/shard_map/all_to_all | solution.py:15
  357.7 5.4 copy-start.3
  357.7 32.6 %all-to-all-start.3 = ((bf16[2,768,768]{2,1,0:T(8,128)(2,1)}), bf16[2,768,768]{2,1,0:T(8,128)(2,1)}, u32[]{:S(2)}, u32[]{:S(2)}) async-start(bf16[2,768,768]{2,1,0:T(8,128)(2,1)} %broadcast_in_dim.84), calls=%async_computation.3 | async-start | bytes 4718592 | tf_op jit(solution)/shard_map/all_to_all | solution.py:15
  366.6 23.7 %copy-start.10 = (bf16[768,640]{0,1:T(8,128)(2,1)S(1)}, bf16[768,640]{0,1:T(8,128)(2,1)}, u32[]{:S(2)}) copy-start(bf16[768,640]{0,1:T(8,128)(2,1)} %copy.45) | copy-start | bytes 2949124
  391.7 3.9 copy-start.25
  391.7 26.1 %all-to-all-start.4 = ((bf16[2,768,640]{1,2,0:T(8,128)(2,1)}), bf16[2,768,640]{1,2,0:T(8,128)(2,1)S(1)}, u32[]{:S(2)}, u32[]{:S(2)}) async-start(bf16[2,768,640]{1,2,0:T(8,128)(2,1)} %broadcast_in_dim.85), calls=%async_computation.4 | async-start | bytes 3932160 | tf_op jit(solution)/shard_map/all_to_all | solution.py:15
  395.6 22.2 %copy-start.12 = (bf16[384,768]{1,0:T(8,128)(2,1)S(1)}, bf16[384,768]{1,0:T(8,128)(2,1)}, u32[]{:S(2)}) copy-start(bf16[384,768]{1,0:T(8,128)(2,1)} %get-tuple-element.35) | copy-start | bytes 1769476
  400.6 25.8 %copy-start.30 = (bf16[1,384,768]{2,1,0:T(8,128)(2,1)}, bf16[1,384,768]{2,1,0:T(8,128)(2,1)S(1)}, u32[]{:S(2)}) copy-start(bf16[1,384,768]{2,1,0:T(8,128)(2,1)S(1)} %get-tuple-element.46) | copy-start | bytes 1769476
  400.6 22.9 %copy-start.24 = (f32[768]{0:T(1024)S(1)}, f32[768]{0:T(1024)}, u32[]{:S(2)}) copy-start(f32[768]{0:T(1024)} %get-tuple-element.13) | copy-start | bytes 9220
  417.8 5.7 copy-start.13
  419.0 274.0 %all-to-all-start.5 = ((bf16[2,384,768]{2,1,0:T(8,128)(2,1)}), bf16[2,384,768]{2,1,0:T(8,128)(2,1)}, u32[]{:S(2)}, u32[]{:S(2)}) async-start(bf16[2,384,768]{2,1,0:T(8,128)(2,1)} %broadcast_in_dim.86), calls=%async_computation.5 | async-start | bytes 2359296 | tf_op jit(solution)/shard_map/all_to_all | solution.py:15
  423.4 261.9 %all-reduce.5.cloned.1.call-start = ((), (), s32[]{:S(2)}) async-start(), calls=%async_computation.8 | async-start | bytes 786432 | tf_op jit(solution)/shard_map/psum | solution.py:37
  426.4 7.8 copy-start.8
  426.4 7.8 copy-start.26
  428.3 260.7 %collective-permute-start.2 = (bf16[384,2,128]{0,2,1:T(8,128)(2,1)}, bf16[384,2,128]{0,2,1:T(8,128)(2,1)}, u32[]{:S(2)}, u32[]{:S(2)}) collective-permute-start(bf16[384,2,128]{0,2,1:T(8,128)(2,1)} %get-tuple-element.24), channel_id=1, source_target_pairs={{0,1},{1,2},{2,3},{3,4},{4,5},{5,6},{6,7},{7,8},{8,9},{9,10},{10,1... | collective-permute-start | bytes 589832 | tf_op jit(solution)/shard_map/ppermute | solution.py:32
  432.2 305.3 %collective-permute-start.3 = (bf16[384,2,128]{0,2,1:T(8,128)(2,1)}, bf16[384,2,128]{0,2,1:T(8,128)(2,1)}, u32[]{:S(2)}, u32[]{:S(2)}) collective-permute-start(bf16[384,2,128]{0,2,1:T(8,128)(2,1)} %get-tuple-element.22), channel_id=1, source_target_pairs={{0,1},{1,2},{2,3},{3,4},{4,5},{5,6},{6,7},{7,8},{8,9},{9,10},{10,1... | collective-permute-start | bytes 589832 | tf_op jit(solution)/shard_map/ppermute | solution.py:32
  685.3 3.6 copy-start.7
  695.8 5.0 copy-start.16
  695.8 33.3 %all-to-all-start.6 = ((bf16[2,768,768]{1,2,0:T(8,128)(2,1)}), bf16[2,768,768]{1,2,0:T(8,128)(2,1)}, u32[]{:S(2)}, u32[]{:S(2)}) async-start(bf16[2,768,768]{1,2,0:T(8,128)(2,1)} %broadcast_in_dim.87), calls=%async_computation.6 | async-start | bytes 4718592 | tf_op jit(solution)/shard_map/all_to_all | solution.py:15
  732.1 5.4 copy-start.2
  732.1 32.6 %all-to-all-start.7 = ((bf16[2,768,768]{2,1,0:T(8,128)(2,1)}), bf16[2,768,768]{2,1,0:T(8,128)(2,1)}, u32[]{:S(2)}, u32[]{:S(2)}) async-start(bf16[2,768,768]{2,1,0:T(8,128)(2,1)} %broadcast_in_dim.88), calls=%async_computation.7 | async-start | bytes 4718592 | tf_op jit(solution)/shard_map/all_to_all | solution.py:15
  (14 other events, 24.4 us)
Sparse Core Ops, SparseCore 0:
  55.4 255.4 all-reduce.6
  434.2 251.0 all-reduce.4
where the time goes:
time: 779 us; the launch traced here: 777 us
  waiting for transfers between devices  612 us (79%)
  matrix products  50.9 us (7%)
  starting transfers between devices  50.1 us (6%)
  local copies, waits for them, and re-layouts  33.8 us (4%)
  other arithmetic  16.3 us (2%)
  between operations  14 us (2%)
    psum x2, waiting for transfers between devices, from_root(): return lax.psum(jnp.where(mine, value, jnp.zeros_like(value)), axis)  502 us
    all_to_all x8, waiting for transfers between devices, from_everyone(): return lax.all_to_all(copies, axis, split_axis=0, concat_axis=0, tiled=True)  110 us
    all_to_all x8, starting transfers between devices, from_everyone(): return lax.all_to_all(copies, axis, split_axis=0, concat_axis=0, tiled=True)  38.4 us
    broadcast_in_dim x8, local copies, waits for them, and re-layouts, from_everyone(): copies = jnp.broadcast_to(value, (lax.axis_size(axis), *value.shape))  16.7 us
  transfers between devices with their start and end apart: 14, of which 8 were waited for; matrix products, arithmetic and copies ran while one was open for 11% of the time, Pallas kernels for 0%

commit v1 on v0

v1 whole, which is shorter than its diff:
```python
import functools
import math

import jax
import jax.numpy as jnp
from jax import lax
from jax.experimental import pallas as pl
from jax.experimental.pallas import tpu as pltpu
from jax.sharding import PartitionSpec as P

HEAD = 128
RATIO = 3
S = 384
D = 768
G = (RATIO + 2) * HEAD
BOTH = ("tm", "mp")
COUNT = 256
BF = jnp.bfloat16
F32 = jnp.float32
QSCALE = 1.0 / (math.sqrt(HEAD) * math.log(2.0))


def place(i):
    return (i >> 7) * 2 + (i & 1), (i >> 2) & 3, (i >> 4) & 7, (i >> 1) & 1


def index(x, y, z, c):
    return ((x >> 1) << 7) | (z << 4) | (y << 2) | (c << 1) | (x & 1)


def pairs(fn):
    return [(i, index(*fn(*place(i)))) for i in range(COUNT)]


ALL4 = (0, 1, 2, 3)
ALL8 = tuple(range(8))


def zodd(z):
    return ((((z + 1) & 7) ^ 1) - 1) & 7


def among(to, xs=ALL4, ys=ALL4, zs=ALL8):
    return [
        (i, j)
        for i, j in pairs(to)
        if place(i)[0] in xs and place(i)[1] in ys and place(i)[2] in zs
    ]


def go_x1(x, y, z, c):
    return x ^ 1, y, z, c


def go_x3(x, y, z, c):
    return x ^ 3, y, z, c


def go_y1(x, y, z, c):
    return x, y ^ 1, z, c


def go_y3(x, y, z, c):
    return x, y ^ 3, z, c


def go_z1(x, y, z, c):
    return x, y, z ^ 1, c


def go_z7(x, y, z, c):
    return x, y, zodd(z), c


X1, X3, Y1, Y3 = pairs(go_x1), pairs(go_x3), pairs(go_y1), pairs(go_y3)
CORE = pairs(lambda x, y, z, c: (x, y, z, 1 - c))
NEXT = [(i, i + 1) for i in range(COUNT - 1)]


def send(v, p):
    return lax.ppermute(v, BOTH, p)


def spread_first(x):
    me = lax.axis_index(BOTH)
    px, py, pz, pc = (me >> 7) * 2 + (me & 1), (me >> 2) & 3, (me >> 4) & 7, (me >> 1) & 1
    half = D // 2
    cur = jnp.where(pc == 0, x[:, :half], send(x[:, half:], CORE))
    got = send(cur[192:], among(go_y3, (0,), (0, 3), (0,)))
    cur = jnp.where(py == 0, cur[:192], got)
    got = send(cur[96:], among(go_y1, (0,), ALL4, (0,)))
    cur = jnp.where((py == 0) | (py == 3), cur[:96], got)
    got = send(cur[48:], among(go_x1, (0, 1), ALL4, (0,)))
    cur = jnp.where(px == 0, cur[:48], got)
    got = send(cur, among(go_x3, ALL4, ALL4, (0,)))
    cur = jnp.where(px < 2, cur, got)
    for i, up, down in ((1, go_z1, go_z7), (2, go_z7, go_z1), (3, go_z1, go_z7)):
        a = send(cur, among(up, ALL4, ALL4, (i - 1, i)))
        b = send(cur, among(down, ALL4, ALL4, ((9 - i) % 8, 8 - i)))
        cur = jnp.where(pz == i, a, jnp.where(pz == 8 - i, b, cur))
    got = send(cur, among(go_z7, ALL4, ALL4, (3, 4)))
    cur = jnp.where(pz == 4, got, cur)
    cur = jnp.concatenate([cur, send(cur, X1)], axis=0)
    cur = jnp.concatenate([cur, send(cur, Y1)], axis=0)
    cur = jnp.concatenate([cur, send(cur, Y3)], axis=0)
    got = send(cur, CORE)
    return jnp.where(
        pc == 0, jnp.concatenate([cur, got], axis=1), jnp.concatenate([got, cur], axis=1)
    )


VMEM = pl.BlockSpec(memory_space=pltpu.VMEM)
SMEM = pl.BlockSpec(memory_space=pltpu.SMEM)
ANY = pl.BlockSpec(memory_space=pl.ANY)
HBM = pl.BlockSpec(memory_space=pltpu.HBM)
NQ, NO, NU = 192, 96, 192
ROWS = NQ + NO + 2 * NU


def params():
    return pltpu.CompilerParams(vmem_limit_bytes=48 << 20)


def cost(flops, nbytes):
    return pl.CostEstimate(flops=flops, bytes_accessed=nbytes, transcendentals=0)


def cut_kernel(l, info, wq, wo, wu, wd, p0, p1, stage, sems):
    core = info[0]
    loads = []
    for j in range(2):
        at = 0
        for i, (src, n) in enumerate(((wq, NQ), (wo, NO), (wu, NU), (wd, NU))):
            rows = pl.ds(pl.multiple_of(core * (2 * n) + j * n, 16), n)
            to = stage.at[j, pl.ds(at, n), pl.ds(0, src.shape[2])]
            c = pltpu.make_async_copy(src.at[l, rows], to, sems.at[4 * j + i])
            c.start()
            loads.append(c)
            at += n
    stores = []
    for j, out in enumerate((p0, p1)):
        for c in loads[4 * j : 4 * j + 4]:
            c.wait()
        c = pltpu.make_async_copy(stage.at[j], out, sems.at[8 + j])
        c.start()
        stores.append(c)
    for c in stores:
        c.wait()


def cut(l, info, weights):
    return pl.pallas_call(
        functools.partial(cut_kernel, l),
        out_shape=[jax.ShapeDtypeStruct((ROWS, D), BF)] * 2,
        in_specs=[SMEM] + [HBM] * 4,
        out_specs=[HBM] * 2,
        scratch_shapes=[pltpu.VMEM((2, ROWS, D), BF), pltpu.SemaphoreType.DMA((10,))],
        compiler_params=params(),
        name="cut",
    )(info, *weights)


def fetch(p):
    a = send(p[0], X1)
    b = send(p[1], X3)
    return a, b, send(a, CORE), send(b, CORE)


def fill(info, quarters, at, n, dst, base, sems, first):
    width = dst.shape[1]
    copies = []
    for j, ref in enumerate(quarters):
        who = info[0] if j < 2 else 1 - info[0]
        row = pl.multiple_of(base + who * (2 * n) + (j % 2) * n, 16)
        c = pltpu.make_async_copy(
            ref.at[pl.ds(at, n), pl.ds(0, width)], dst.at[pl.ds(row, n)], sems.at[first + j]
        )
        c.start()
        copies.append(c)
    return copies


def bring(src, dst, sem):
    c = pltpu.make_async_copy(src, dst, sem)
    c.start()
    return c


def wait(copies):
    for c in copies:
        c.wait()


def rms(t, gain):
    scale = lax.rsqrt(jnp.mean(t * t, axis=-1, keepdims=True) + 1e-06)
    return (t * scale * gain).astype(BF)


def dot(a, b):
    return jnp.dot(a, b, preferred_element_type=F32)


def dot_t(a, b):
    return lax.dot_general(a, b, (((1,), (1,)), ((), ())), preferred_element_type=F32)


def head_norm(t):
    return t * lax.rsqrt(jnp.mean(t * t, axis=-1, keepdims=True) + 1e-06)


def open_qkv(l, info, wq, quarters, w, sems):
    return [bring(wq.at[l], w.at[pl.ds(0, D)], sems.at[4])] + fill(
        info, quarters, 0, NQ, w, D, sems, 0
    )


def scales(info, temps, l, g):
    group = info[2] if g == 0 else 1 - info[2]
    return [temps[l, group * RATIO + r] * QSCALE for r in range(RATIO)]


def project(h, w, ts, q_ref, kv_ref, row, g, keys):
    n = h.shape[0]
    first = 0 if ts is not None else RATIO * HEAD
    last = G if keys else RATIO * HEAD
    raw = dot(h, w[pl.ds(g * D, D), first:last])
    if ts is not None:
        for r in range(RATIO):
            t = head_norm(raw[:, r * HEAD : (r + 1) * HEAD])
            q_ref[pl.ds((g * RATIO + r) * S + row, n), :] = (t * ts[r]).astype(BF)
    if keys:
        at = RATIO * HEAD - first
        kv_ref[pl.ds(row, n), pl.ds(g * 2 * HEAD, HEAD)] = head_norm(
            raw[:, at : at + HEAD]
        ).astype(BF)
        kv_ref[pl.ds(row, n), pl.ds(g * 2 * HEAD + HEAD, HEAD)] = raw[:, at + HEAD :].astype(BF)


QKV_STEP = 192
MIX_STEP = 192
END_STEP = 192


def qkv_kernel(l, info, temps, x_ref, gain, wq, a, b, d, e, q_ref, kv_ref, w, sems):
    copies = open_qkv(l, info, wq, (a, b, d, e), w, sems)
    copies[0].wait()
    hs = []
    for row in range(0, S, QKV_STEP):
        h = rms(x_ref[pl.ds(row, QKV_STEP), :].astype(F32), gain[pl.ds(l, 1), :])
        project(h, w, scales(info, temps, l, 0), q_ref, kv_ref, row, 0, True)
        hs.append(h)
    wait(copies[1:])
    for i, h in enumerate(hs):
        project(h, w, scales(info, temps, l, 1), q_ref, kv_ref, i * QKV_STEP, 1, True)


KV_SHAPE = jax.ShapeDtypeStruct((S, 4 * HEAD), BF)
Q_SHAPE = (2 * RATIO * S, HEAD)
QKV_SCRATCH = [pltpu.VMEM((2 * D, G), BF), pltpu.SemaphoreType.DMA((5,))]


def qkv(l, info, temps, x, gain, wq, quarters):
    return pl.pallas_call(
        functools.partial(qkv_kernel, l),
        out_shape=[jax.ShapeDtypeStruct(Q_SHAPE, BF), KV_SHAPE],
        in_specs=[SMEM, SMEM, VMEM, VMEM] + [HBM] * 5,
        out_specs=[VMEM, VMEM],
        scratch_shapes=QKV_SCRATCH,
        compiler_params=params(),
        cost_estimate=cost(4 * S * D * G, 3 << 20),
        name="qkv",
    )(info, temps, x, gain, wq, *quarters)


def first_kv_kernel(l, info, x_ref, gain, wq, a, b, d, e, kv_ref, w, sems):
    copies = open_qkv(l, info, wq, (a, b, d, e), w, sems)
    hs = []
    for row in range(0, S, QKV_STEP):
        hs.append(rms(x_ref[pl.ds(row, QKV_STEP), :].astype(F32), gain[pl.ds(l, 1), :]))
    wait(copies)
    for g in range(2):
        for i, h in enumerate(hs):
            project(h, w, None, None, kv_ref, i * QKV_STEP, g, True)


def first_kv(l, info, x, gain, wq, quarters):
    return pl.pallas_call(
        functools.partial(first_kv_kernel, l),
        out_shape=KV_SHAPE,
        in_specs=[SMEM, VMEM, VMEM] + [HBM] * 5,
        out_specs=VMEM,
        scratch_shapes=QKV_SCRATCH,
        compiler_params=params(),
        cost_estimate=cost(8 * S * D * HEAD, 3 << 20),
        name="first_kv",
    )(info, x, gain, wq, *quarters)


def mix(q_ref, kvs, columns, shuts, o_ref, ext, g):
    for i, (kv, at) in enumerate(zip(kvs, columns)):
        ext[i, :, :HEAD] = kv[:, at + HEAD : at + 2 * HEAD]
        ext[i, :, HEAD:] = jnp.ones((S, HEAD), BF)
    for r in range(RATIO):
        for row in range(0, S, MIX_STEP):
            q = q_ref[pl.ds((g * RATIO + r) * S + row, MIX_STEP), :]
            scores = [dot_t(q, kv[:, at : at + HEAD]) for kv, at in zip(kvs, columns)]
            tops = [s.max(axis=-1, keepdims=True) for s in scores]
            top = tops[0]
            for t, shut in zip(tops[1:], shuts[1:]):
                top = jnp.maximum(top, t - shut)
            acc = None
            for i, s in enumerate(scores):
                base = top if i == 0 else top + shuts[i]
                part = dot(jnp.exp2(s - base).astype(BF), ext[i])
                acc = part if acc is None else acc + part
            o_ref[pl.ds(row, MIX_STEP), pl.ds((g * RATIO + r) * HEAD, HEAD)] = (
                acc[:, :HEAD] / acc[:, HEAD:]
            ).astype(BF)


def attend_kernel(info, q, kv, prior, first, o_ref, ext):
    shuts = [None, jnp.where(info[1] >= 1, 0.0, 1e30), jnp.where(info[1] >= 2, 0.0, 1e30)]
    for g in range(2):
        mine, theirs = g * 2 * HEAD, (1 - g) * 2 * HEAD
        mix(q, (kv, prior, first), (mine, theirs, mine), shuts, o_ref, ext, g)


def attend(info, q, kv, prior, first):
    return pl.pallas_call(
        attend_kernel,
        out_shape=jax.ShapeDtypeStruct((S, D), BF),
        in_specs=[SMEM] + [VMEM] * 4,
        out_specs=VMEM,
        scratch_shapes=[pltpu.VMEM((3, S, 2 * HEAD), BF)],
        compiler_params=params(),
        cost_estimate=cost(4 * S * 3 * S * D, 4 << 20),
        name="attend",
    )(info, q, kv, prior, first)


def first_mix_kernel(info, temps, x_ref, kv, gain, wq, a, b, d, e, o_ref, w, sems, q, ext):
    copies = open_qkv(0, info, wq, (a, b, d, e), w, sems)
    hs = []
    for row in range(0, S, QKV_STEP):
        hs.append(rms(x_ref[pl.ds(row, QKV_STEP), :].astype(F32), gain[pl.ds(0, 1), :]))
    wait(copies)
    for g in range(2):
        for i, h in enumerate(hs):
            project(h, w, scales(info, temps, 0, g), q, None, i * QKV_STEP, g, False)
        mix(q, (kv,), (g * 2 * HEAD,), [None], o_ref, ext, g)


def first_mix(info, temps, x, kv, gain, wq, quarters):
    return pl.pallas_call(
        first_mix_kernel,
        out_shape=jax.ShapeDtypeStruct((S, D), BF),
        in_specs=[SMEM] * 2 + [VMEM] * 3 + [HBM] * 5,
        out_specs=VMEM,
        scratch_shapes=QKV_SCRATCH
        + [pltpu.VMEM(Q_SHAPE, BF), pltpu.VMEM((1, S, 2 * HEAD), BF)],
        compiler_params=params(),
        cost_estimate=cost(4 * S * S * D + 4 * S * D * 3 * HEAD, 4 << 20),
        name="first_mix",
    )(info, temps, x, kv, gain, wq, *quarters)


def finish_kernel(
    l, info, x_ref, o_ref, gain, wo, wu, wd, a, b, d, e, out, back, up, down, sems
):
    quarters = (a, b, d, e)
    copies = [bring(wo.at[l], back.at[pl.ds(0, S)], sems.at[12])]
    copies += fill(info, quarters, NQ, NO, back, S, sems, 0)
    more = [bring(wu.at[l], up.at[pl.ds(0, D)], sems.at[13])]
    more += fill(info, quarters, NQ + NO, NU, up, D, sems, 4)
    more += [bring(wd.at[l], down.at[pl.ds(0, D)], sems.at[14])]
    more += fill(info, quarters, NQ + NO + NU, NU, down, D, sems, 8)
    wait(copies)
    for n, row in enumerate(range(0, S, END_STEP)):
        rows = pl.ds(row, END_STEP)
        x = (x_ref[rows, :].astype(F32) + dot(o_ref[rows, :], back[...])).astype(BF)
        h = rms(x.astype(F32), gain[pl.ds(l, 1), :])
        if n == 0:
            wait(more)
        y = x.astype(F32)
        for g in range(2):
            t = jax.nn.gelu(dot(h, up[pl.ds(g * D, D), :]), approximate=True).astype(BF)
            y = y + dot(t, down[pl.ds(g * D, D), :])
        out[rows, :] = y.astype(BF)


def finish(l, info, x, o, gain, own, quarters):
    return pl.pallas_call(
        functools.partial(finish_kernel, l),
        out_shape=jax.ShapeDtypeStruct((S, D), BF),
        in_specs=[SMEM] + [VMEM] * 3 + [HBM] * 7,
        out_specs=VMEM,
        scratch_shapes=[
            pltpu.VMEM((D, D), BF),
            pltpu.VMEM((2 * D, D), BF),
            pltpu.VMEM((2 * D, D), BF),
            pltpu.SemaphoreType.DMA((15,)),
        ],
        compiler_params=params(),
        cost_estimate=cost(2 * S * D * (D + 4 * D), 9 << 20),
        name="finish",
    )(info, x, o, gain, *own, *quarters)


def shards(x, gain_a, wqkv, temps, wout, gain_m, wup, wdown):
    me = lax.axis_index(BOTH)
    info = jnp.stack([(me >> 1) & 1, me, me & 1]).astype(jnp.int32)
    x = x[0]
    own = (wout, wup, wdown)
    p = cut(0, info, (wqkv, *own))
    xb, p = lax.optimization_barrier((x, p))
    w0 = fetch(p)
    first = spread_first(xb)
    p = cut(1, info, (wqkv, *own))
    p, _ = lax.optimization_barrier((p, w0[1]))
    w1 = fetch(p)

    q, kv = qkv(0, info, temps, x, gain_a, wqkv, w0)
    prior = send(kv, NEXT)
    kv0 = first_kv(0, info, first, gain_a, wqkv, w0)
    o = attend(info, q, kv, prior, kv0)
    x = finish(0, info, x, o, gain_m, own, w0)
    q, kv = qkv(1, info, temps, x, gain_a, wqkv, w1)
    prior = send(kv, NEXT)
    o = first_mix(info, temps, first, kv0, gain_a, wqkv, w0)
    first = finish(0, info, first, o, gain_m, own, w0)
    kv0 = first_kv(1, info, first, gain_a, wqkv, w1)
    o = attend(info, q, kv, prior, kv0)
    return finish(1, info, x, o, gain_m, own, w1)[None]


def solution(mesh):
    in_specs = (
        P(BOTH, None, None),
        P(),
        P(None, None, "mp"),
        P(),
        P(None, "mp", None),
        P(),
        P(None, None, "mp"),
        P(None, "mp", None),
    )
    return jax.shard_map(
        shards, mesh=mesh, in_specs=in_specs, out_specs=P(BOTH, None, None), check_vma=False
    )
```

time: 779 us -> 162 us (0.21)
  waiting for transfers between devices: 612 us -> 57.8 us
  Pallas kernels: 0 us -> 53 us
  matrix products: 50.9 us -> 0 us
  local copies, waits for them, and re-layouts: 33.8 us -> 8.18 us
  starting transfers between devices: 50.1 us -> 36.2 us
  between operations: 14 us -> 0.69 us
  other arithmetic: 16.3 us -> 3.2 us
    psum x2 -> x0, waiting for transfers between devices: 502 us -> none  [from_root(): return lax.psum(jnp.where(mine, value, jnp.zeros_like(value)), axis)]
    all_to_all x8 -> x0, waiting for transfers between devices: 110 us -> none  [from_everyone(): return lax.all_to_all(copies, axis, split_axis=0, concat_axis=0, tiled=True)]
    ppermute x4 -> x26, waiting for transfers between devices: 0.01 us -> 57.8 us  [send(): return lax.ppermute(v, BOTH, p)]
    pallas_call x0 -> x12, Pallas kernels: none -> 53 us  [the longest x3 18.8 us: finish(): pl.pallas_call(functools.partial(finish_kernel, l), out_shape=jax.ShapeDt...]
    dot_general x18 -> x0, matrix products: 50.9 us -> none  [the longest x2 10.4 us: layer_by_weights(): jnp.einsum('fsc,cd->fsd', block, collect(down_local, 'mp', 0), preferred_...]
    all_to_all x8 -> x0, starting transfers between devices: 38.4 us -> none  [from_everyone(): return lax.all_to_all(copies, axis, split_axis=0, concat_axis=0, tiled=True)]
    ppermute x4 -> x26, starting transfers between devices: 11.6 us -> 36.2 us  [send(): return lax.ppermute(v, BOTH, p)]
    broadcast_in_dim x8 -> x0, local copies, waits for them, and re-layouts: 16.7 us -> none  [from_everyone(): copies = jnp.broadcast_to(value, (lax.axis_size(axis), *value.shape))]
  transfers between devices with their start and end apart: 14 -> 26, of which waited for: 8 -> 10; matrix products, arithmetic and copies ran while one was open for 11% -> 1% of each run, Pallas kernels for 0% -> 21%
where the time goes in v1:
time: 162 us; the launch traced here: 159 us
  waiting for transfers between devices  57.8 us (36%)
  Pallas kernels  53 us (33%)
  starting transfers between devices  36.2 us (22%)
  local copies, waits for them, and re-layouts  8.18 us (5%)
  other arithmetic  3.2 us (2%)
    ppermute x26, waiting for transfers between devices, send(): return lax.ppermute(v, BOTH, p)  57.8 us
    ppermute x26, starting transfers between devices, send(): return lax.ppermute(v, BOTH, p)  36.2 us
    pallas_call x3, Pallas kernels, finish(): pl.pallas_call(functools.partial(finish_kernel, l), out_shape=jax.ShapeDt...  18.8 us
    pallas_call x2, Pallas kernels, attend(): pl.pallas_call(attend_kernel, out_shape=jax.ShapeDtypeStruct((S, D), BF),...  12.4 us
    unnamed x28, local copies, waits for them, and re-layouts  7.46 us
    pallas_call x2, Pallas kernels, qkv(): pl.pallas_call(functools.partial(qkv_kernel, l), out_shape=[jax.ShapeDtyp...  6.46 us
    pallas_call x2, Pallas kernels, cut(): pl.pallas_call(functools.partial(cut_kernel, l), out_shape=[jax.ShapeDtyp...  5.29 us
    pallas_call x1, Pallas kernels, first_mix(): pl.pallas_call(first_mix_kernel, out_shape=jax.ShapeDtypeStruct((S, D), B...  5.26 us
  transfers between devices with their start and end apart: 26, of which 10 were waited for; matrix products, arithmetic and copies ran while one was open for 1% of the time, Pallas kernels for 21%

profile of v1, /device:TPU:8, one launch (start us, length us, event | category | flops | bytes accessed | tf_op | source)
XLA Modules:
  0.0 159.1 jit_solution(16960655910746224513)
XLA Ops:
  0.1 1.5 copy-done
  2.9 2.6 %cut.2 = (bf16[672,768]{1,0:T(8,128)(2,1)S(1)}, bf16[672,768]{1,0:T(8,128)(2,1)S(1)}) custom-call(s32[3]{0:T(128)S(1)} %pad_add_fusion.info, bf16[2,768,640]{2,1,0:T(8,128)(2,1)S(1)} %copy-done, bf16[2,384,768]{2,1,0:T(8,128)(2,1)S(1)} %copy-done.2, bf16[2,768,768]{2,1,0:T(8,128)(2,1)} %wu.9, bf16[2,768,768]{2,1,0:T(8,128)(2,1)} %wd.9), custom_call_target="tpu_custom_call" | custom-call | tf_op jit(solution)/shard_map/cut/pallas_call | solution.py:152
  7.7 1.7 %collective-permute-done.5 = bf16[384,384]{1,0:T(8,128)(2,1)} collective-permute-done((bf16[384,384]{1,0:T(8,128)(2,1)S(1)}, bf16[384,384]{1,0:T(8,128)(2,1)}, u32[]{:S(2)}, u32[]{:S(2)}) %collective-permute-start.5) | collective-permute-done | bytes 294944 | tf_op jit(solution)/shard_map/ppermute | solution.py:81
  14.0 11.2 %collective-permute-start.7 = (bf16[96,384]{1,0:T(8,128)(2,1)S(1)}, bf16[96,384]{1,0:T(8,128)(2,1)S(1)}, u32[]{:S(2)}, u32[]{:S(2)}) collective-permute-start(bf16[96,384]{1,0:T(8,128)(2,1)S(1)} %slice.35), channel_id=1, source_target_pairs={{0,4},{2,6},{4,0},{6,2},{8,12},{10,14},{12,8},{14,10}} | collective-permute-start | bytes 221192 | tf_op jit(solution)/shard_map/ppermute | solution.py:81
  25.3 2.2 %collective-permute-done.7 = bf16[96,384]{1,0:T(8,128)(2,1)S(1)} collective-permute-done((bf16[96,384]{1,0:T(8,128)(2,1)S(1)}, bf16[96,384]{1,0:T(8,128)(2,1)S(1)}, u32[]{:S(2)}, u32[]{:S(2)}) %collective-permute-start.7) | collective-permute-done | bytes 73760 | tf_op jit(solution)/shard_map/ppermute | solution.py:81
  28.4 1.9 %collective-permute-start.8 = (bf16[48,384]{1,0:T(8,128)(2,1)S(1)}, bf16[48,384]{1,0:T(8,128)(2,1)S(1)}, u32[]{:S(2)}, u32[]{:S(2)}) collective-permute-start(bf16[48,384]{1,0:T(8,128)(2,1)S(1)} %slice.37), channel_id=1, source_target_pairs={{0,1},{1,0},{2,3},{3,2},{4,5},{5,4},{6,7},{7,6},{8,9},{9,8},{10,11... | collective-permute-start | bytes 110600 | tf_op jit(solution)/shard_map/ppermute | solution.py:81
  30.4 2.1 %collective-permute-start = (bf16[672,768]{1,0:T(8,128)(2,1)}, bf16[672,768]{1,0:T(8,128)(2,1)}, u32[]{:S(2)}, u32[]{:S(2)}) collective-permute-start(bf16[672,768]{1,0:T(8,128)(2,1)} %copy-done.9), channel_id=1, source_target_pairs={{0,1},{1,0},{2,3},{3,2},{4,5},{5,4},{6,7},{7,6},{8,9},{9,8},{10,11... | collective-permute-start | bytes 3096584 | tf_op jit(solution)/shard_map/ppermute | solution.py:81
  32.5 2.2 %collective-permute-done.8 = bf16[48,384]{1,0:T(8,128)(2,1)S(1)} collective-permute-done((bf16[48,384]{1,0:T(8,128)(2,1)S(1)}, bf16[48,384]{1,0:T(8,128)(2,1)S(1)}, u32[]{:S(2)}, u32[]{:S(2)}) %collective-permute-start.8) | collective-permute-done | bytes 36896 | tf_op jit(solution)/shard_map/ppermute | solution.py:81
  34.7 1.9 %collective-permute-start.9 = (bf16[48,384]{1,0:T(8,128)(2,1)S(1)}, bf16[48,384]{1,0:T(8,128)(2,1)S(1)}, u32[]{:S(2)}, u32[]{:S(2)}) collective-permute-start(bf16[48,384]{1,0:T(8,128)(2,1)S(1)} %slice_select_fusion.3), channel_id=1, source_target_pairs={{0,129},{1,128},{2,131},{3,130},{4,133},{5,132},{6,135},{7,134},{8... | collective-permute-start | bytes 110600 | tf_op jit(solution)/shard_map/ppermute | solution.py:81
  36.6 14.7 %collective-permute-done.9 = bf16[48,384]{1,0:T(8,128)(2,1)S(1)} collective-permute-done((bf16[48,384]{1,0:T(8,128)(2,1)S(1)}, bf16[48,384]{1,0:T(8,128)(2,1)S(1)}, u32[]{:S(2)}, u32[]{:S(2)}) %collective-permute-start.9) | collective-permute-done | bytes 36896 | tf_op jit(solution)/shard_map/ppermute | solution.py:81
  51.3 1.9 %collective-permute-start.11 = (bf16[48,384]{1,0:T(8,128)(2,1)S(1)}, bf16[48,384]{1,0:T(8,128)(2,1)S(1)}, u32[]{:S(2)}, u32[]{:S(2)}) collective-permute-start(bf16[48,384]{1,0:T(8,128)(2,1)S(1)} %broadcast_select_fusion), channel_id=1, source_target_pairs={{0,112},{1,113},{2,114},{3,115},{4,116},{5,117},{6,118},{7,119},{8... | collective-permute-start | bytes 110600 | tf_op jit(solution)/shard_map/ppermute | solution.py:81
  53.2 1.9 %collective-permute-start.10 = (bf16[48,384]{1,0:T(8,128)(2,1)S(1)}, bf16[48,384]{1,0:T(8,128)(2,1)S(1)}, u32[]{:S(2)}, u32[]{:S(2)}) collective-permute-start(bf16[48,384]{1,0:T(8,128)(2,1)S(1)} %broadcast_select_fusion), channel_id=1, source_target_pairs={{0,16},{1,17},{2,18},{3,19},{4,20},{5,21},{6,22},{7,23},{8,24},{9,... | collective-permute-start | bytes 110600 | tf_op jit(solution)/shard_map/ppermute | solution.py:81
  55.2 3.2 %collective-permute-done.11 = bf16[48,384]{1,0:T(8,128)(2,1)S(1)} collective-permute-done((bf16[48,384]{1,0:T(8,128)(2,1)S(1)}, bf16[48,384]{1,0:T(8,128)(2,1)S(1)}, u32[]{:S(2)}, u32[]{:S(2)}) %collective-permute-start.11) | collective-permute-done | bytes 36896 | tf_op jit(solution)/shard_map/ppermute | solution.py:81
  60.5 2.6 %cut.3 = (bf16[672,768]{1,0:T(8,128)(2,1)S(1)}, bf16[672,768]{1,0:T(8,128)(2,1)S(1)}) custom-call(s32[3]{0:T(128)S(1)} %pad_add_fusion.info, bf16[2,768,640]{2,1,0:T(8,128)(2,1)S(1)} %copy-done.1, bf16[2,384,768]{2,1,0:T(8,128)(2,1)S(1)} %copy-done.3, bf16[2,768,768]{2,1,0:T(8,128)(2,1)} %wu.9, bf16[2,768,768]{2,1,0:T(8,128)(2,1)} %wd.9), custom_call_target="tpu_custom_call" | custom-call | tf_op jit(solution)/shard_map/cut/pallas_call | solution.py:152
  68.3 1.7 %collective-permute-start.17 = (bf16[48,384]{1,0:T(8,128)(2,1)S(1)}, bf16[48,384]{1,0:T(8,128)(2,1)S(1)}, u32[]{:S(2)}, u32[]{:S(2)}) collective-permute-start(bf16[48,384]{1,0:T(8,128)(2,1)S(1)} %broadcast_select_fusion.1), channel_id=1, source_target_pairs={{0,1},{1,0},{2,3},{3,2},{4,5},{5,4},{6,7},{7,6},{8,9},{9,8},{10,11... | collective-permute-start | bytes 110600 | tf_op jit(solution)/shard_map/ppermute | solution.py:81
  70.0 18.1 %collective-permute-done.17 = bf16[48,384]{1,0:T(8,128)(2,1)S(1)} collective-permute-done((bf16[48,384]{1,0:T(8,128)(2,1)S(1)}, bf16[48,384]{1,0:T(8,128)(2,1)S(1)}, u32[]{:S(2)}, u32[]{:S(2)}) %collective-permute-start.17) | collective-permute-done | bytes 36896 | tf_op jit(solution)/shard_map/ppermute | solution.py:81
  88.7 3.8 %collective-permute-done.18 = bf16[96,384]{1,0:T(8,128)(2,1)S(1)} collective-permute-done((bf16[96,384]{1,0:T(8,128)(2,1)S(1)}, bf16[96,384]{1,0:T(8,128)(2,1)S(1)}, u32[]{:S(2)}, u32[]{:S(2)}) %collective-permute-start.18) | collective-permute-done | bytes 73760 | tf_op jit(solution)/shard_map/ppermute | solution.py:81
  92.5 1.7 %collective-permute-start.19 = (bf16[192,384]{1,0:T(8,128)(2,1)S(1)}, bf16[192,384]{1,0:T(8,128)(2,1)S(1)}, u32[]{:S(2)}, u32[]{:S(2)}) collective-permute-start(bf16[192,384]{1,0:T(8,128)(2,1)S(1)} %pad_maximum_fusion.1), channel_id=1, source_target_pairs={{0,12},{1,13},{2,14},{3,15},{4,8},{5,9},{6,10},{7,11},{8,4},{9,5},... | collective-permute-start | bytes 442376 | tf_op jit(solution)/shard_map/ppermute | solution.py:81
  94.7 3.0 %collective-permute-done.19 = bf16[192,384]{1,0:T(8,128)(2,1)S(1)} collective-permute-done((bf16[192,384]{1,0:T(8,128)(2,1)S(1)}, bf16[192,384]{1,0:T(8,128)(2,1)S(1)}, u32[]{:S(2)}, u32[]{:S(2)}) %collective-permute-start.19) | collective-permute-done | bytes 147488 | tf_op jit(solution)/shard_map/ppermute | solution.py:81
  97.9 3.2 %qkv.2 = (bf16[2304,128]{1,0:T(8,128)(2,1)S(1)}, bf16[384,512]{1,0:T(8,128)(2,1)S(1)}) custom-call(s32[3]{0:T(128)S(1)} %pad_add_fusion.info, f32[2,6]{1,0:T(2,128)S(1)} %copy-done.8, bf16[384,768]{1,0:T(8,128)(2,1)S(1)} %bitcast.7, f32[2,768]{1,0:T(2,128)S(1)} %copy-done.6, bf16[2,768,640]{2,1,0:T(8,128)(2,1)} %wq.13, ...), custom_call_target="tpu_custom_call" | custom-call | flops 754974720 | bytes 3145728 | tf_op jit(solution)/shard_map/qkv/pallas_call | solution.py:263
  101.2 2.4 %collective-permute-start.4 = (bf16[384,512]{1,0:T(8,128)(2,1)S(1)}, bf16[384,512]{1,0:T(8,128)(2,1)S(1)}, u32[]{:S(2)}, u32[]{:S(2)}) collective-permute-start(bf16[384,512]{1,0:T(8,128)(2,1)S(1)} %get-tuple-element.23.kv), channel_id=1, source_target_pairs={{0,1},{1,2},{2,3},{3,4},{4,5},{5,6},{6,7},{7,8},{8,9},{9,10},{10,1... | collective-permute-start | bytes 1179656 | tf_op jit(solution)/shard_map/ppermute | solution.py:81
  103.7 2.5 %first_kv.2.first.kv = bf16[384,512]{1,0:T(8,128)(2,1)S(1)} custom-call(s32[3]{0:T(128)S(1)} %pad_add_fusion.info, bf16[384,768]{1,0:T(8,128)(2,1)S(1)} %maximum_select_fusion.x_ref, f32[2,768]{1,0:T(2,128)S(1)} %copy-done.6, bf16[2,768,640]{2,1,0:T(8,128)(2,1)} %wq.13, bf16[672,768]{1,0:T(8,128)(2,1)} %collective-permute-done.a, ...), custom_call_target="tpu_custom_call" | custom-call | flops 301989888 | bytes 3145728 | tf_op jit(solution)/shard_map/first_kv/pallas_call | solution.py:287
  106.2 8.2 %collective-permute-done.4.prior = bf16[384,512]{1,0:T(8,128)(2,1)S(1)} collective-permute-done((bf16[384,512]{1,0:T(8,128)(2,1)S(1)}, bf16[384,512]{1,0:T(8,128)(2,1)S(1)}, u32[]{:S(2)}, u32[]{:S(2)}) %collective-permute-start.4) | collective-permute-done | bytes 393248 | tf_op jit(solution)/shard_map/ppermute | solution.py:81
  114.4 6.2 %attend.2.o_ref = bf16[384,768]{1,0:T(8,128)(2,1)S(1)} custom-call(s32[3]{0:T(128)S(1)} %pad_add_fusion.info, bf16[2304,128]{1,0:T(8,128)(2,1)S(1)} %get-tuple-element.22.q, bf16[384,512]{1,0:T(8,128)(2,1)S(1)} %get-tuple-element.23.kv, bf16[384,512]{1,0:T(8,128)(2,1)S(1)} %collective-permute-done.4.prior, bf16[384,512]{1,0:T(8,128)(2,1)S(1)} %first_kv.2.first.kv), custom_call_target="tpu_custom_call" | custom-call | flops 1358954496 | bytes 4194304 | tf_op jit(solution)/shard_map/attend/pallas_call | solution.py:329
  120.6 6.0 %finish.3.x_ref = bf16[384,768]{1,0:T(8,128)(2,1)S(1)} custom-call(s32[3]{0:T(128)S(1)} %pad_add_fusion.info, bf16[384,768]{1,0:T(8,128)(2,1)S(1)} %bitcast.8, bf16[384,768]{1,0:T(8,128)(2,1)S(1)} %attend.2.o_ref, f32[2,768]{1,0:T(2,128)S(1)} %copy-done.7, bf16[2,384,768]{2,1,0:T(8,128)(2,1)} %wo.9, bf16[2,768,768]{2,1,0:T(8,128)(2,1)} %wu.9, ...), custom_call_target="tpu_custom_call" | custom-call | flops 2264924160 | bytes 9437184 | tf_op jit(solution)/shard_map/finish/pallas_call | solution.py:392
  126.6 3.2 %qkv.3 = (bf16[2304,128]{1,0:T(8,128)(2,1)S(1)}, bf16[384,512]{1,0:T(8,128)(2,1)S(1)}) custom-call(s32[3]{0:T(128)S(1)} %pad_add_fusion.info, f32[2,6]{1,0:T(2,128)S(1)} %copy-done.8, bf16[384,768]{1,0:T(8,128)(2,1)S(1)} %finish.3.x_ref, f32[2,768]{1,0:T(2,128)S(1)} %copy-done.6, bf16[2,768,640]{2,1,0:T(8,128)(2,1)} %wq.13, ...), custom_call_target="tpu_custom_call" | custom-call | flops 754974720 | bytes 3145728 | tf_op jit(solution)/shard_map/qkv/pallas_call | solution.py:263
  129.8 2.4 %collective-permute-start.25 = (bf16[384,512]{1,0:T(8,128)(2,1)S(1)}, bf16[384,512]{1,0:T(8,128)(2,1)S(1)}, u32[]{:S(2)}, u32[]{:S(2)}) collective-permute-start(bf16[384,512]{1,0:T(8,128)(2,1)S(1)} %get-tuple-element.30.kv), channel_id=1, source_target_pairs={{0,1},{1,2},{2,3},{3,4},{4,5},{5,6},{6,7},{7,8},{8,9},{9,10},{10,1... | collective-permute-start | bytes 1179656 | tf_op jit(solution)/shard_map/ppermute | solution.py:81
  132.2 5.3 %first_mix.1.o_ref = bf16[384,768]{1,0:T(8,128)(2,1)S(1)} custom-call(s32[3]{0:T(128)S(1)} %pad_add_fusion.info, f32[2,6]{1,0:T(2,128)S(1)} %copy-done.8, bf16[384,768]{1,0:T(8,128)(2,1)S(1)} %maximum_select_fusion.x_ref, bf16[384,512]{1,0:T(8,128)(2,1)S(1)} %first_kv.2.first.kv, f32[2,768]{1,0:T(2,128)S(1)} %copy-done.6, bf16[2,768,640]{2,1,0:T(8,128)(2,1)} %wq.13, ...), custom_call_target="tpu_custom_call" | custom-call | flops 905969664 | bytes 4194304 | tf_op jit(solution)/shard_map/first_mix/pallas_call | solution.py:354
  137.5 6.0 %finish.4.x_ref = bf16[384,768]{1,0:T(8,128)(2,1)S(1)} custom-call(s32[3]{0:T(128)S(1)} %pad_add_fusion.info, bf16[384,768]{1,0:T(8,128)(2,1)S(1)} %maximum_select_fusion.x_ref, bf16[384,768]{1,0:T(8,128)(2,1)S(1)} %first_mix.1.o_ref, f32[2,768]{1,0:T(2,128)S(1)} %copy-done.7, bf16[2,384,768]{2,1,0:T(8,128)(2,1)} %wo.9, bf16[2,768,768]{2,1,0:T(8,128)(2,1)} %wu.9, ...), custom_call_target="tpu_custom_call" | custom-call | flops 2264924160 | bytes 9437184 | tf_op jit(solution)/shard_map/finish/pallas_call | solution.py:392
  143.4 2.4 %first_kv.3.first = bf16[384,512]{1,0:T(8,128)(2,1)S(1)} custom-call(s32[3]{0:T(128)S(1)} %pad_add_fusion.info, bf16[384,768]{1,0:T(8,128)(2,1)S(1)} %finish.4.x_ref, f32[2,768]{1,0:T(2,128)S(1)} %copy-done.6, bf16[2,768,640]{2,1,0:T(8,128)(2,1)} %wq.13, bf16[672,768]{1,0:T(8,128)(2,1)S(1)} %collective-permute-done.21.a, ...), custom_call_target="tpu_custom_call" | custom-call | flops 301989888 | bytes 3145728 | tf_op jit(solution)/shard_map/first_kv/pallas_call | solution.py:287
  145.9 6.2 %attend.3.o_ref = bf16[384,768]{1,0:T(8,128)(2,1)S(1)} custom-call(s32[3]{0:T(128)S(1)} %pad_add_fusion.info, bf16[2304,128]{1,0:T(8,128)(2,1)S(1)} %get-tuple-element.29.q, bf16[384,512]{1,0:T(8,128)(2,1)S(1)} %get-tuple-element.30.kv, bf16[384,512]{1,0:T(8,128)(2,1)S(1)} %collective-permute-done.25.prior, bf16[384,512]{1,0:T(8,128)(2,1)S(1)} %first_kv.3.first), custom_call_target="tpu_custom_call" | custom-call | flops 1358954496 | bytes 4194304 | tf_op jit(solution)/shard_map/attend/pallas_call | solution.py:329
  152.1 6.8 %finish.5 = bf16[384,768]{1,0:T(8,128)(2,1)} custom-call(s32[3]{0:T(128)S(1)} %pad_add_fusion.info, bf16[384,768]{1,0:T(8,128)(2,1)S(1)} %finish.3.x_ref, bf16[384,768]{1,0:T(8,128)(2,1)S(1)} %attend.3.o_ref, f32[2,768]{1,0:T(2,128)S(1)} %copy-done.7, bf16[2,384,768]{2,1,0:T(8,128)(2,1)} %wo.9, bf16[2,768,768]{2,1,0:T(8,128)(2,1)} %wu.9, ...), custom_call_target="tpu_custom_call" | custom-call | flops 2264924160 | bytes 9437184 | tf_op jit(solution)/shard_map/finish/pallas_call | solution.py:392
  (78 shorter events, 17.6 us)
Async XLA Ops:
  2.9 57.6 %copy-start.3 = (bf16[2,384,768]{2,1,0:T(8,128)(2,1)S(1)}, bf16[2,384,768]{2,1,0:T(8,128)(2,1)}, u32[]{:S(2)}) copy-start(bf16[2,384,768]{2,1,0:T(8,128)(2,1)} %wo.9) | copy-start | bytes 3538948
  7.5 1.8 %collective-permute-start.5 = (bf16[384,384]{1,0:T(8,128)(2,1)S(1)}, bf16[384,384]{1,0:T(8,128)(2,1)}, u32[]{:S(2)}, u32[]{:S(2)}) collective-permute-start(bf16[384,384]{1,0:T(8,128)(2,1)S(1)} %slice.25), channel_id=1, source_target_pairs={{0,2},{1,3},{2,0},{3,1},{4,6},{5,7},{6,4},{7,5},{8,10},{9,11},{10,... | collective-permute-start | bytes 884744 | tf_op jit(solution)/shard_map/ppermute | solution.py:81
  7.7 52.8 %copy-start.1 = (bf16[2,768,640]{2,1,0:T(8,128)(2,1)S(1)}, bf16[2,768,640]{2,1,0:T(8,128)(2,1)}, u32[]{:S(2)}) copy-start(bf16[2,768,640]{2,1,0:T(8,128)(2,1)} %wq.13) | copy-start | bytes 5898244
  11.0 1.3 collective-permute-start.6
  14.0 13.5 %collective-permute-start.7 = (bf16[96,384]{1,0:T(8,128)(2,1)S(1)}, bf16[96,384]{1,0:T(8,128)(2,1)S(1)}, u32[]{:S(2)}, u32[]{:S(2)}) collective-permute-start(bf16[96,384]{1,0:T(8,128)(2,1)S(1)} %slice.35), channel_id=1, source_target_pairs={{0,4},{2,6},{4,0},{6,2},{8,12},{10,14},{12,8},{14,10}} | collective-permute-start | bytes 221192 | tf_op jit(solution)/shard_map/ppermute | solution.py:81
  25.2 39.9 %collective-permute-start.1 = (bf16[672,768]{1,0:T(8,128)(2,1)}, bf16[672,768]{1,0:T(8,128)(2,1)}, u32[]{:S(2)}, u32[]{:S(2)}) collective-permute-start(bf16[672,768]{1,0:T(8,128)(2,1)} %copy-done.10), channel_id=1, source_target_pairs={{0,129},{1,128},{2,131},{3,130},{4,133},{5,132},{6,135},{7,134},{8... | collective-permute-start | bytes 3096584 | tf_op jit(solution)/shard_map/ppermute | solution.py:81
  28.4 6.2 %collective-permute-start.8 = (bf16[48,384]{1,0:T(8,128)(2,1)S(1)}, bf16[48,384]{1,0:T(8,128)(2,1)S(1)}, u32[]{:S(2)}, u32[]{:S(2)}) collective-permute-start(bf16[48,384]{1,0:T(8,128)(2,1)S(1)} %slice.37), channel_id=1, source_target_pairs={{0,1},{1,0},{2,3},{3,2},{4,5},{5,4},{6,7},{7,6},{8,9},{9,8},{10,11... | collective-permute-start | bytes 110600 | tf_op jit(solution)/shard_map/ppermute | solution.py:81
  30.4 36.7 %collective-permute-start = (bf16[672,768]{1,0:T(8,128)(2,1)}, bf16[672,768]{1,0:T(8,128)(2,1)}, u32[]{:S(2)}, u32[]{:S(2)}) collective-permute-start(bf16[672,768]{1,0:T(8,128)(2,1)} %copy-done.9), channel_id=1, source_target_pairs={{0,1},{1,0},{2,3},{3,2},{4,5},{5,4},{6,7},{7,6},{8,9},{9,8},{10,11... | collective-permute-start | bytes 3096584 | tf_op jit(solution)/shard_map/ppermute | solution.py:81
  34.7 16.6 %collective-permute-start.9 = (bf16[48,384]{1,0:T(8,128)(2,1)S(1)}, bf16[48,384]{1,0:T(8,128)(2,1)S(1)}, u32[]{:S(2)}, u32[]{:S(2)}) collective-permute-start(bf16[48,384]{1,0:T(8,128)(2,1)S(1)} %slice_select_fusion.3), channel_id=1, source_target_pairs={{0,129},{1,128},{2,131},{3,130},{4,133},{5,132},{6,135},{7,134},{8... | collective-permute-start | bytes 110600 | tf_op jit(solution)/shard_map/ppermute | solution.py:81
  51.3 7.1 %collective-permute-start.11 = (bf16[48,384]{1,0:T(8,128)(2,1)S(1)}, bf16[48,384]{1,0:T(8,128)(2,1)S(1)}, u32[]{:S(2)}, u32[]{:S(2)}) collective-permute-start(bf16[48,384]{1,0:T(8,128)(2,1)S(1)} %broadcast_select_fusion), channel_id=1, source_target_pairs={{0,112},{1,113},{2,114},{3,115},{4,116},{5,117},{6,118},{7,119},{8... | collective-permute-start | bytes 110600 | tf_op jit(solution)/shard_map/ppermute | solution.py:81
  53.2 5.9 %collective-permute-start.10 = (bf16[48,384]{1,0:T(8,128)(2,1)S(1)}, bf16[48,384]{1,0:T(8,128)(2,1)S(1)}, u32[]{:S(2)}, u32[]{:S(2)}) collective-permute-start(bf16[48,384]{1,0:T(8,128)(2,1)S(1)} %broadcast_select_fusion), channel_id=1, source_target_pairs={{0,16},{1,17},{2,18},{3,19},{4,20},{5,21},{6,22},{7,23},{8,24},{9,... | collective-permute-start | bytes 110600 | tf_op jit(solution)/shard_map/ppermute | solution.py:81
  59.1 6.4 %collective-permute-start.13 = (bf16[48,384]{1,0:T(8,128)(2,1)S(1)}, bf16[48,384]{1,0:T(8,128)(2,1)S(1)}, u32[]{:S(2)}, u32[]{:S(2)}) collective-permute-start(bf16[48,384]{1,0:T(8,128)(2,1)S(1)} %select_select_fusion.2), channel_id=1, source_target_pairs={{96,112},{97,113},{98,114},{99,115},{100,116},{101,117},{102,118},... | collective-permute-start | bytes 110600 | tf_op jit(solution)/shard_map/ppermute | solution.py:81
  59.8 5.8 %collective-permute-start.12 = (bf16[48,384]{1,0:T(8,128)(2,1)S(1)}, bf16[48,384]{1,0:T(8,128)(2,1)S(1)}, u32[]{:S(2)}, u32[]{:S(2)}) collective-permute-start(bf16[48,384]{1,0:T(8,128)(2,1)S(1)} %select_select_fusion.2), channel_id=1, source_target_pairs={{16,32},{17,33},{18,34},{19,35},{20,36},{21,37},{22,38},{23,39},{2... | collective-permute-start | bytes 110600 | tf_op jit(solution)/shard_map/ppermute | solution.py:81
  65.1 32.8 %copy-start.6 = (f32[2,768]{1,0:T(2,128)S(1)}, f32[2,768]{1,0:T(2,128)}, u32[]{:S(2)}) copy-start(f32[2,768]{1,0:T(2,128)} %gain.14) | copy-start | bytes 18436
  65.1 32.8 %copy-start.8 = (f32[2,6]{1,0:T(2,128)S(1)}, f32[2,6]{1,0:T(2,128)}, u32[]{:S(2)}) copy-start(f32[2,6]{1,0:T(2,128)} %temps.5) | copy-start | bytes 148
  65.2 29.1 %collective-permute-start.21 = (bf16[672,768]{1,0:T(8,128)(2,1)}, bf16[672,768]{1,0:T(8,128)(2,1)S(1)}, u32[]{:S(2)}, u32[]{:S(2)}) collective-permute-start(bf16[672,768]{1,0:T(8,128)(2,1)} %copy-done.12), channel_id=1, source_target_pairs={{0,1},{1,0},{2,3},{3,2},{4,5},{5,4},{6,7},{7,6},{8,9},{9,8},{10,11... | collective-permute-start | bytes 3096584 | tf_op jit(solution)/shard_map/ppermute | solution.py:81
  65.2 29.1 %collective-permute-start.22 = (bf16[672,768]{1,0:T(8,128)(2,1)}, bf16[672,768]{1,0:T(8,128)(2,1)}, u32[]{:S(2)}, u32[]{:S(2)}) collective-permute-start(bf16[672,768]{1,0:T(8,128)(2,1)} %copy-done.11), channel_id=1, source_target_pairs={{0,129},{1,128},{2,131},{3,130},{4,133},{5,132},{6,135},{7,134},{8... | collective-permute-start | bytes 3096584 | tf_op jit(solution)/shard_map/ppermute | solution.py:81
  65.6 1.4 collective-permute-start.15
  66.2 1.3 collective-permute-start.14
  66.9 31.0 %collective-permute-start.3 = (bf16[672,768]{1,0:T(8,128)(2,1)}, bf16[672,768]{1,0:T(8,128)(2,1)S(1)}, u32[]{:S(2)}, u32[]{:S(2)}) collective-permute-start(bf16[672,768]{1,0:T(8,128)(2,1)} %collective-permute-done.1.b), channel_id=1, source_target_pairs={{0,2},{1,3},{2,0},{3,1},{4,6},{5,7},{6,4},{7,5},{8,10},{9,11},{10,... | collective-permute-start | bytes 3096584 | tf_op jit(solution)/shard_map/ppermute | solution.py:81
  67.0 30.9 %collective-permute-start.2 = (bf16[672,768]{1,0:T(8,128)(2,1)}, bf16[672,768]{1,0:T(8,128)(2,1)S(1)}, u32[]{:S(2)}, u32[]{:S(2)}) collective-permute-start(bf16[672,768]{1,0:T(8,128)(2,1)} %collective-permute-done.a), channel_id=1, source_target_pairs={{0,2},{1,3},{2,0},{3,1},{4,6},{5,7},{6,4},{7,5},{8,10},{9,11},{10,... | collective-permute-start | bytes 3096584 | tf_op jit(solution)/shard_map/ppermute | solution.py:81
  67.5 0.7 collective-permute-start.16
  68.2 29.7 %copy-start.5 = (bf16[1,384,768]{2,1,0:T(8,128)(2,1)S(1)}, bf16[1,384,768]{2,1,0:T(8,128)(2,1)}, u32[]{:S(2)}) copy-start(bf16[1,384,768]{2,1,0:T(8,128)(2,1)} %param.8) | copy-start | bytes 1769476
  68.3 19.8 %collective-permute-start.17 = (bf16[48,384]{1,0:T(8,128)(2,1)S(1)}, bf16[48,384]{1,0:T(8,128)(2,1)S(1)}, u32[]{:S(2)}, u32[]{:S(2)}) collective-permute-start(bf16[48,384]{1,0:T(8,128)(2,1)S(1)} %broadcast_select_fusion.1), channel_id=1, source_target_pairs={{0,1},{1,0},{2,3},{3,2},{4,5},{5,4},{6,7},{7,6},{8,9},{9,8},{10,11... | collective-permute-start | bytes 110600 | tf_op jit(solution)/shard_map/ppermute | solution.py:81
  88.1 4.4 %collective-permute-start.18 = (bf16[96,384]{1,0:T(8,128)(2,1)S(1)}, bf16[96,384]{1,0:T(8,128)(2,1)S(1)}, u32[]{:S(2)}, u32[]{:S(2)}) collective-permute-start(bf16[96,384]{1,0:T(8,128)(2,1)S(1)} %pad_maximum_fusion.2), channel_id=1, source_target_pairs={{0,4},{1,5},{2,6},{3,7},{4,0},{5,1},{6,2},{7,3},{8,12},{9,13},{10,... | collective-permute-start | bytes 221192 | tf_op jit(solution)/shard_map/ppermute | solution.py:81
  92.5 5.2 %collective-permute-start.19 = (bf16[192,384]{1,0:T(8,128)(2,1)S(1)}, bf16[192,384]{1,0:T(8,128)(2,1)S(1)}, u32[]{:S(2)}, u32[]{:S(2)}) collective-permute-start(bf16[192,384]{1,0:T(8,128)(2,1)S(1)} %pad_maximum_fusion.1), channel_id=1, source_target_pairs={{0,12},{1,13},{2,14},{3,15},{4,8},{5,9},{6,10},{7,11},{8,4},{9,5},... | collective-permute-start | bytes 442376 | tf_op jit(solution)/shard_map/ppermute | solution.py:81
  94.2 32.4 %collective-permute-start.23 = (bf16[672,768]{1,0:T(8,128)(2,1)S(1)}, bf16[672,768]{1,0:T(8,128)(2,1)S(1)}, u32[]{:S(2)}, u32[]{:S(2)}) collective-permute-start(bf16[672,768]{1,0:T(8,128)(2,1)S(1)} %collective-permute-done.21.a), channel_id=1, source_target_pairs={{0,2},{1,3},{2,0},{3,1},{4,6},{5,7},{6,4},{7,5},{8,10},{9,11},{10,... | collective-permute-start | bytes 3096584 | tf_op jit(solution)/shard_map/ppermute | solution.py:81
  94.2 32.4 %collective-permute-start.24 = (bf16[672,768]{1,0:T(8,128)(2,1)}, bf16[672,768]{1,0:T(8,128)(2,1)S(1)}, u32[]{:S(2)}, u32[]{:S(2)}) collective-permute-start(bf16[672,768]{1,0:T(8,128)(2,1)} %collective-permute-done.22.b), channel_id=1, source_target_pairs={{0,2},{1,3},{2,0},{3,1},{4,6},{5,7},{6,4},{7,5},{8,10},{9,11},{10,... | collective-permute-start | bytes 3096584 | tf_op jit(solution)/shard_map/ppermute | solution.py:81
  97.8 5.8 %collective-permute-start.20 = (bf16[384,384]{1,0:T(8,128)(2,1)S(1)}, bf16[384,384]{1,0:T(8,128)(2,1)S(1)}, u32[]{:S(2)}, u32[]{:S(2)}) collective-permute-start(bf16[384,384]{1,0:T(8,128)(2,1)S(1)} %pad_maximum_fusion), channel_id=1, source_target_pairs={{0,2},{1,3},{2,0},{3,1},{4,6},{5,7},{6,4},{7,5},{8,10},{9,11},{10,... | collective-permute-start | bytes 884744 | tf_op jit(solution)/shard_map/ppermute | solution.py:81
  101.2 13.2 %collective-permute-start.4 = (bf16[384,512]{1,0:T(8,128)(2,1)S(1)}, bf16[384,512]{1,0:T(8,128)(2,1)S(1)}, u32[]{:S(2)}, u32[]{:S(2)}) collective-permute-start(bf16[384,512]{1,0:T(8,128)(2,1)S(1)} %get-tuple-element.23.kv), channel_id=1, source_target_pairs={{0,1},{1,2},{2,3},{3,4},{4,5},{5,6},{6,7},{7,8},{8,9},{9,10},{10,1... | collective-permute-start | bytes 1179656 | tf_op jit(solution)/shard_map/ppermute | solution.py:81
  114.4 6.2 %copy-start.7 = (f32[2,768]{1,0:T(2,128)S(1)}, f32[2,768]{1,0:T(2,128)}, u32[]{:S(2)}) copy-start(f32[2,768]{1,0:T(2,128)} %gain.15) | copy-start | bytes 18436
  129.8 16.0 %collective-permute-start.25 = (bf16[384,512]{1,0:T(8,128)(2,1)S(1)}, bf16[384,512]{1,0:T(8,128)(2,1)S(1)}, u32[]{:S(2)}, u32[]{:S(2)}) collective-permute-start(bf16[384,512]{1,0:T(8,128)(2,1)S(1)} %get-tuple-element.30.kv), channel_id=1, source_target_pairs={{0,1},{1,2},{2,3},{3,4},{4,5},{5,6},{6,7},{7,8},{8,9},{9,10},{10,1... | collective-permute-start | bytes 1179656 | tf_op jit(solution)/shard_map/ppermute | solution.py:81
  (8 other events, 12.1 us)
